TPU v7x, 32 devices: a whole 2x2x4 slice. The times are simulated.
32 devices in a mesh: trc: 4 (over z), lat: 4 (over y, x), lon: 2 (over core).
Axes of the slice: x: 2, y: 2, z: 4, core: 2. Of those that a mesh axis runs over, the one named last changes fastest.
Arguments:
- tracers: float32 [8, 16, 128, 128], P('trc', 'lat', 'lon'), may hold values from -6 to 6
- land_mask: int32 [16, 128], P('lat', 'lon'), may hold values 0 or 1
- bottom_level: int32 [16, 128], P('lat', 'lon'), may hold values from 1 to 128
- bottom_part: float32 [16, 128], P('lat', 'lon'), may hold values from 0.05 to 1
- velocity: float32 [2, 2, 8, 32768], P(None, None, ('lat', 'lon'), 'trc'), may hold values from -0.45 to 0.45
- upwelling: float32 [2, 8, 32768], P(None, ('lat', 'lon'), 'trc'), may hold values from -0.3 to 0.3
- diffusivity: float32 [2, 8, 32768], P(None, ('lat', 'lon'), 'trc'), may hold values from 0.08 to 0.32
Outputs:
- tracers_out: float32 [8, 16, 128, 128], P('trc', 'lat', 'lon')
All inputs are finite; a program needn't handle non-finite values. No bound on the sum of `land_mask` on one device may be relied on, other than what follows from the above.
Results may differ from a plain program's by a relative error of at most 0.0003.
Values sent between devices are 32-bit elements; how exact they have to be, the bound alone decides.
A program may use at most 64 MiB of HBM per device.

v0:
```python
import jax
import jax.numpy as jnp
from jax import lax
from jax.sharding import PartitionSpec as P

STEPS = 2
fraction_floor = 0.25


def with_halo(block, sides, width):
    for axis, dim in sides:
        count = lax.axis_size(axis)
        forward = [(i, i + 1) for i in range(count - 1)]
        backward = [(target, source) for source, target in forward]
        low = lax.ppermute(
            lax.slice_in_dim(block, block.shape[dim] - width, None, axis=dim), axis, forward
        )
        high = lax.ppermute(lax.slice_in_dim(block, 0, width, axis=dim), axis, backward)
        block = jnp.concatenate([low, block, high], axis=dim)
    return block


def minmod(first, second):
    return 0.5 * (jnp.sign(first) + jnp.sign(second)) * jnp.minimum(jnp.abs(first), jnp.abs(second))


def window(array, start, stop, offset):
    return lax.slice_in_dim(array, start, stop, axis=array.ndim + offset)


def face_divergence(field, speed, mixing, fraction, offset):
    extent = field.shape[field.ndim + offset]
    before = window(field, 0, extent - 3, offset)
    lower = window(field, 1, extent - 2, offset)
    upper = window(field, 2, extent - 1, offset)
    after = window(field, 3, extent, offset)
    face_speed = 0.5 * (window(speed, 1, extent - 2, offset) + window(speed, 2, extent - 1, offset))
    face_area = jnp.minimum(
        window(fraction, 1, extent - 2, offset), window(fraction, 2, extent - 1, offset)
    )
    face_mixing = 0.5 * (
        window(mixing, 1, extent - 2, offset) + window(mixing, 2, extent - 1, offset)
    )
    jump = upper - lower
    damping = 0.5 * (1.0 - jnp.abs(face_speed))
    from_lower = lower + damping * minmod(lower - before, jump)
    from_upper = upper - damping * minmod(jump, after - upper)
    face_value = jnp.where(face_speed >= 0.0, from_lower, from_upper)
    face_flux = face_area * (face_speed * face_value - face_mixing * jump)
    return window(face_flux, 1, extent - 3, offset) - window(face_flux, 0, extent - 4, offset)


def substep(field, fraction, eastward, northward, mixing, rising):
    across_rows = face_divergence(field, northward, mixing, fraction, -3)[..., 2:-2, :]
    across_cols = face_divergence(field, eastward, mixing, fraction, -2)[..., 2:-2, :, :]
    centre = field[..., 2:-2, 2:-2, :]
    wet_share = fraction[2:-2, 2:-2, :]
    top_area = jnp.minimum(wet_share[:, :, :-1], wet_share[:, :, 1:])
    lifting = rising[:, :, :-1]
    carried = jnp.where(lifting >= 0.0, centre[..., :-1], centre[..., 1:])
    vertical = top_area * lifting * carried
    closed = jnp.zeros(vertical.shape[:-1] + (1,), jnp.float32)
    across_levels = jnp.concatenate([vertical, closed], axis=-1) - jnp.concatenate(
        [closed, vertical], axis=-1
    )
    return centre - (across_rows + across_cols + across_levels) / jnp.maximum(
        wet_share, fraction_floor
    )


def cell_fraction(land_mask, bottom_level, bottom_part, levels):
    level_index = lax.broadcasted_iota(jnp.int32, land_mask.shape + (levels,), 2)
    deepest = bottom_level[:, :, None] - 1
    full_cell = (level_index < deepest).astype(jnp.float32)
    last_cell = (level_index == deepest).astype(jnp.float32) * bottom_part[:, :, None]
    return land_mask.astype(jnp.float32)[:, :, None] * (full_cell + last_cell)


def body(tracers, land_mask, bottom_level, bottom_part, velocity, upwelling, diffusivity):
    levels = tracers.shape[3]
    block_shape = (tracers.shape[1], tracers.shape[2], levels)
    fraction = cell_fraction(land_mask, bottom_level, bottom_part, levels)
    tracer_count = tracers.shape[0]
    collected = []
    moved = (
        lax.all_gather(velocity, "trc", axis=3, tiled=True),
        lax.all_gather(upwelling, "trc", axis=2, tiled=True),
        lax.all_gather(diffusivity, "trc", axis=2, tiled=True),
    )
    speeds = moved[0].reshape((STEPS, 2) + block_shape)
    rises = moved[1].reshape((STEPS,) + block_shape)
    mixes = moved[2].reshape((STEPS,) + block_shape)
    collected = [
        (speeds[number, 0], speeds[number, 1], mixes[number], rises[number])
        for number in range(STEPS)
    ]
    field = tracers
    wide_frac = fraction
    for number in range(STEPS):
        eastward, northward, mixing, rising = collected[number]
        extras = [fraction[None]] if number == 0 else []
        stack = jnp.concatenate(
            [field] + extras + [jnp.stack([eastward, northward, mixing])], axis=0
        )
        widened = with_halo(stack, (("lat", 1), ("lon", 2)), 2)
        if number == 0:
            wide_frac = widened[tracer_count]
            moved_flows = widened[tracer_count + 1 :]
        else:
            moved_flows = widened[tracer_count:]
        field = substep(
            widened[:tracer_count],
            wide_frac,
            moved_flows[0],
            moved_flows[1],
            moved_flows[2],
            rising,
        )
    return field


def solution(mesh):
    placed = (
        P("trc", "lat", "lon", None),
        P("lat", "lon"),
        P("lat", "lon"),
        P("lat", "lon"),
        P(None, None, ("lat", "lon"), "trc"),
        P(None, ("lat", "lon"), "trc"),
        P(None, ("lat", "lon"), "trc"),
    )
    return jax.shard_map(
        body, mesh=mesh, in_specs=placed, out_specs=P("trc", "lat", "lon", None), check_vma=False
    )
```

profile of v0, /device:TPU:0, one launch (start us, length us, event | category | flops | bytes accessed | tf_op | source)
XLA Modules:
  0.0 89.0 jit_solution(9641395497896303604)
XLA Ops:
  0.0 0.7 convert_element_type.14
  0.7 0.7 broadcast_add_fusion
  1.4 15.8 %all_gather.10 = f32[2,1,32768]{2,1,0:T(1,128)S(1)} all-gather(f32[2,1,8192]{2,1,0:T(1,128)} %param.13), channel_id=1, replica_groups=mesh['trc'=4,'lat'=4,'lon'=2] {'trc'}, dimensions={2}, use_global_device_ids=true | all-gather | bytes 327680 | tf_op jit(solution)/shard_map/all_gather | solution.py:88
  17.3 16.4 %all_gather.9 = f32[2,2,1,32768]{3,2,1,0:T(1,128)S(1)} all-gather(f32[2,2,1,8192]{3,2,1,0:T(1,128)} %param.11), channel_id=1, replica_groups=mesh['trc'=4,'lat'=4,'lon'=2] {'trc'}, dimensions={3}, use_global_device_ids=true | all-gather | bytes 655360 | tf_op jit(solution)/shard_map/all_gather | solution.py:86
  34.0 3.4 %collective-permute-start = (f32[6,2,64,128]{3,2,1,0:T(8,128)S(1)}, f32[6,2,64,128]{3,2,1,0:T(8,128)S(1)}, u32[]{:S(2)}, u32[]{:S(2)}) collective-permute-start(f32[6,2,64,128]{3,2,1,0:T(8,128)S(1)} %get-tuple-element.25), channel_id=1, source_target_pairs={{0,2},{2,4},{4,6},{1,3},{3,5},{5,7},{8,10},{10,12},{12,14},{9,11},... | collective-permute-start | bytes 1179656 | tf_op jit(solution)/shard_map/ppermute | solution.py:15
  37.4 1.3 %collective-permute-start.1 = (f32[6,2,64,128]{3,2,1,0:T(8,128)S(1)}, f32[6,2,64,128]{3,2,1,0:T(8,128)S(1)}, u32[]{:S(2)}, u32[]{:S(2)}) collective-permute-start(f32[6,2,64,128]{3,2,1,0:T(8,128)S(1)} %get-tuple-element.26), channel_id=1, source_target_pairs={{2,0},{4,2},{6,4},{3,1},{5,3},{7,5},{10,8},{12,10},{14,12},{11,9},... | collective-permute-start | bytes 1179656 | tf_op jit(solution)/shard_map/ppermute | solution.py:18
  38.8 13.8 %all_gather.11 = f32[2,1,32768]{2,1,0:T(1,128)S(1)} all-gather(f32[2,1,8192]{2,1,0:T(1,128)S(1)} %copy-done.1), channel_id=1, replica_groups=mesh['trc'=4,'lat'=4,'lon'=2] {'trc'}, dimensions={2}, use_global_device_ids=true | all-gather | bytes 327680 | tf_op jit(solution)/shard_map/all_gather | solution.py:87
  52.7 1.3 %collective-permute-start.2 = (f32[6,8,2,128]{3,2,1,0:T(2,128)S(1)}, f32[6,8,2,128]{3,2,1,0:T(2,128)S(1)}, u32[]{:S(2)}, u32[]{:S(2)}) collective-permute-start(f32[6,8,2,128]{3,2,1,0:T(2,128)S(1)} %get-tuple-element.16), channel_id=1, source_target_pairs={{0,1},{2,3},{4,5},{6,7},{8,9},{10,11},{12,13},{14,15},{16,17},{18,... | collective-permute-start | bytes 147464 | tf_op jit(solution)/shard_map/ppermute | solution.py:15
  54.0 1.3 %collective-permute-start.3 = (f32[6,8,2,128]{3,2,1,0:T(2,128)S(1)}, f32[6,8,2,128]{3,2,1,0:T(2,128)S(1)}, u32[]{:S(2)}, u32[]{:S(2)}) collective-permute-start(f32[6,8,2,128]{3,2,1,0:T(2,128)S(1)} %get-tuple-element.17), channel_id=1, source_target_pairs={{1,0},{3,2},{5,4},{7,6},{9,8},{11,10},{13,12},{15,14},{17,16},{19,... | collective-permute-start | bytes 147464 | tf_op jit(solution)/shard_map/ppermute | solution.py:18
  55.3 1.8 %collective-permute-done.3 = f32[6,8,2,128]{3,2,1,0:T(2,128)S(1)} collective-permute-done((f32[6,8,2,128]{3,2,1,0:T(2,128)S(1)}, f32[6,8,2,128]{3,2,1,0:T(2,128)S(1)}, u32[]{:S(2)}, u32[]{:S(2)}) %collective-permute-start.3) | collective-permute-done | bytes 49184 | tf_op jit(solution)/shard_map/ppermute | solution.py:18
  57.1 0.2 pad_maximum_fusion
  57.8 0.3 subtract_multiply_fusion.3
  58.3 1.0 %subtract_multiply_fusion.1 = f32[2,8,65,128]{3,2,1,0:T(8,128)S(1)} fusion(f32[6,8,2,128]{3,2,1,0:T(2,128)S(1)} %collective-permute-done.3, f32[6,2,64,128]{3,2,1,0:T(8,128)S(1)} %collective-permute-done.1, f32[6,4,64,128]{3,2,1,0:T(8,128)S(1)} %constant_dynamic-update-slice_fusion, f32[6,2,64,128]{3,2,1,0:T(8,128)S(1)} %collective-permute-done, ...), kind=kLoop, calls=%fused_computation.33 | loop fusion | flops 5058560 | bytes 3335168 | tf_op jit(solution)/shard_map/mul | solution.py:49
  59.6 0.2 fusion.24
  59.9 4.6 %collective-permute-start.4 = (f32[5,2,64,128]{3,2,1,0:T(8,128)S(1)}, f32[5,2,64,128]{3,2,1,0:T(8,128)S(1)}, u32[]{:S(2)}, u32[]{:S(2)}) collective-permute-start(f32[5,2,64,128]{3,2,1,0:T(8,128)S(1)} %get-tuple-element.27), channel_id=1, source_target_pairs={{0,2},{2,4},{4,6},{1,3},{3,5},{5,7},{8,10},{10,12},{12,14},{9,11},... | collective-permute-start | bytes 983048 | tf_op jit(solution)/shard_map/ppermute | solution.py:15
  64.5 1.3 %collective-permute-start.5 = (f32[5,2,64,128]{3,2,1,0:T(8,128)S(1)}, f32[5,2,64,128]{3,2,1,0:T(8,128)S(1)}, u32[]{:S(2)}, u32[]{:S(2)}) collective-permute-start(f32[5,2,64,128]{3,2,1,0:T(8,128)S(1)} %get-tuple-element.28), channel_id=1, source_target_pairs={{2,0},{4,2},{6,4},{3,1},{5,3},{7,5},{10,8},{12,10},{14,12},{11,9},... | collective-permute-start | bytes 983048 | tf_op jit(solution)/shard_map/ppermute | solution.py:18
  65.8 5.9 %collective-permute-done.4 = f32[5,2,64,128]{3,2,1,0:T(8,128)S(1)} collective-permute-done((f32[5,2,64,128]{3,2,1,0:T(8,128)S(1)}, f32[5,2,64,128]{3,2,1,0:T(8,128)S(1)}, u32[]{:S(2)}, u32[]{:S(2)}) %collective-permute-start.4) | collective-permute-done | bytes 327712 | tf_op jit(solution)/shard_map/ppermute | solution.py:15
  71.7 9.8 %collective-permute-done.5 = f32[5,2,64,128]{3,2,1,0:T(8,128)S(1)} collective-permute-done((f32[5,2,64,128]{3,2,1,0:T(8,128)S(1)}, f32[5,2,64,128]{3,2,1,0:T(8,128)S(1)}, u32[]{:S(2)}, u32[]{:S(2)}) %collective-permute-start.5) | collective-permute-done | bytes 327712 | tf_op jit(solution)/shard_map/ppermute | solution.py:18
  81.6 1.3 %collective-permute-start.6 = (f32[5,8,2,128]{3,2,1,0:T(2,128)S(1)}, f32[5,8,2,128]{3,2,1,0:T(2,128)S(1)}, u32[]{:S(2)}, u32[]{:S(2)}) collective-permute-start(f32[5,8,2,128]{3,2,1,0:T(2,128)S(1)} %get-tuple-element.23), channel_id=1, source_target_pairs={{0,1},{2,3},{4,5},{6,7},{8,9},{10,11},{12,13},{14,15},{16,17},{18,... | collective-permute-start | bytes 122888 | tf_op jit(solution)/shard_map/ppermute | solution.py:15
  82.9 1.3 %collective-permute-start.7 = (f32[5,8,2,128]{3,2,1,0:T(2,128)S(1)}, f32[5,8,2,128]{3,2,1,0:T(2,128)S(1)}, u32[]{:S(2)}, u32[]{:S(2)}) collective-permute-start(f32[5,8,2,128]{3,2,1,0:T(2,128)S(1)} %get-tuple-element.24), channel_id=1, source_target_pairs={{1,0},{3,2},{5,4},{7,6},{9,8},{11,10},{13,12},{15,14},{17,16},{19,... | collective-permute-start | bytes 122888 | tf_op jit(solution)/shard_map/ppermute | solution.py:18
  84.3 1.7 %collective-permute-done.7 = f32[5,8,2,128]{3,2,1,0:T(2,128)S(1)} collective-permute-done((f32[5,8,2,128]{3,2,1,0:T(2,128)S(1)}, f32[5,8,2,128]{3,2,1,0:T(2,128)S(1)}, u32[]{:S(2)}, u32[]{:S(2)}) %collective-permute-start.7) | collective-permute-done | bytes 40992 | tf_op jit(solution)/shard_map/ppermute | solution.py:18
  86.5 0.3 subtract_multiply_fusion.2
  87.0 1.0 %subtract_multiply_fusion = f32[2,8,65,128]{3,2,1,0:T(8,128)S(1)} fusion(f32[5,8,2,128]{3,2,1,0:T(2,128)S(1)} %collective-permute-done.7, f32[5,2,64,128]{3,2,1,0:T(8,128)S(1)} %collective-permute-done.5, f32[1,4,64,128]{3,2,1,0:T(8,128)S(1)} %bitcast.48, f32[1,4,64,128]{3,2,1,0:T(8,128)S(1)} %get-tuple-element.34, ...), kind=kLoop, calls=%fused_computation.29 | loop fusion | flops 6656000 | bytes 3056640 | tf_op jit(solution)/shard_map/mul | solution.py:49
  88.1 0.9 %fusion.20 = f32[2,4,64,128]{3,2,1,0:T(8,128)} fusion(f32[2,4,64,128]{3,2,1,0:T(8,128)S(1)} %fusion.24, f32[2,8,64,128]{3,2,1,0:T(8,128)S(1)} %get-tuple-element.30, f32[2,8,64,128]{3,2,1,0:T(8,128)S(1)} %get-tuple-element.29, f32[2,4,68,128]{3,2,1,0:T(8,128)S(1)} %get-tuple-element.36, f32[2,4,68,128]{3,2,1,0:T(8,128)S(1)} %get-tuple-element.35, ...), kind=kLoop, calls=%fused_computation.70 | loop fusion | flops 458752 | bytes 1964032 | tf_op jit(solution)/shard_map/sub | solution.py:66
  (46 shorter events, 2.1 us)
Async XLA Ops:
  0.0 33.7 %copy-start = (f32[2,4,64,128]{3,2,1,0:T(8,128)S(1)}, f32[2,4,64,128]{3,2,1,0:T(8,128)}, u32[]{:S(2)}) copy-start(f32[2,4,64,128]{3,2,1,0:T(8,128)} %param.7) | copy-start | bytes 786436
  0.0 33.7 %copy-start.2 = (f32[4,64]{1,0:T(4,128)S(1)}, f32[4,64]{1,0:T(4,128)}, u32[]{:S(2)}) copy-start(f32[4,64]{1,0:T(4,128)} %param.10) | copy-start | bytes 3076
  33.7 5.1 %copy-start.1 = (f32[2,1,8192]{2,1,0:T(1,128)S(1)}, f32[2,1,8192]{2,1,0:T(1,128)}, u32[]{:S(2)}) copy-start(f32[2,1,8192]{2,1,0:T(1,128)} %param.12) | copy-start | bytes 196612
  34.0 18.6 %collective-permute-start = (f32[6,2,64,128]{3,2,1,0:T(8,128)S(1)}, f32[6,2,64,128]{3,2,1,0:T(8,128)S(1)}, u32[]{:S(2)}, u32[]{:S(2)}) collective-permute-start(f32[6,2,64,128]{3,2,1,0:T(8,128)S(1)} %get-tuple-element.25), channel_id=1, source_target_pairs={{0,2},{2,4},{4,6},{1,3},{3,5},{5,7},{8,10},{10,12},{12,14},{9,11},... | collective-permute-start | bytes 1179656 | tf_op jit(solution)/shard_map/ppermute | solution.py:15
  37.4 15.2 %collective-permute-start.1 = (f32[6,2,64,128]{3,2,1,0:T(8,128)S(1)}, f32[6,2,64,128]{3,2,1,0:T(8,128)S(1)}, u32[]{:S(2)}, u32[]{:S(2)}) collective-permute-start(f32[6,2,64,128]{3,2,1,0:T(8,128)S(1)} %get-tuple-element.26), channel_id=1, source_target_pairs={{2,0},{4,2},{6,4},{3,1},{5,3},{7,5},{10,8},{12,10},{14,12},{11,9},... | collective-permute-start | bytes 1179656 | tf_op jit(solution)/shard_map/ppermute | solution.py:18
  52.7 2.6 %collective-permute-start.2 = (f32[6,8,2,128]{3,2,1,0:T(2,128)S(1)}, f32[6,8,2,128]{3,2,1,0:T(2,128)S(1)}, u32[]{:S(2)}, u32[]{:S(2)}) collective-permute-start(f32[6,8,2,128]{3,2,1,0:T(2,128)S(1)} %get-tuple-element.16), channel_id=1, source_target_pairs={{0,1},{2,3},{4,5},{6,7},{8,9},{10,11},{12,13},{14,15},{16,17},{18,... | collective-permute-start | bytes 147464 | tf_op jit(solution)/shard_map/ppermute | solution.py:15
  54.0 3.1 %collective-permute-start.3 = (f32[6,8,2,128]{3,2,1,0:T(2,128)S(1)}, f32[6,8,2,128]{3,2,1,0:T(2,128)S(1)}, u32[]{:S(2)}, u32[]{:S(2)}) collective-permute-start(f32[6,8,2,128]{3,2,1,0:T(2,128)S(1)} %get-tuple-element.17), channel_id=1, source_target_pairs={{1,0},{3,2},{5,4},{7,6},{9,8},{11,10},{13,12},{15,14},{17,16},{19,... | collective-permute-start | bytes 147464 | tf_op jit(solution)/shard_map/ppermute | solution.py:18
  59.9 11.8 %collective-permute-start.4 = (f32[5,2,64,128]{3,2,1,0:T(8,128)S(1)}, f32[5,2,64,128]{3,2,1,0:T(8,128)S(1)}, u32[]{:S(2)}, u32[]{:S(2)}) collective-permute-start(f32[5,2,64,128]{3,2,1,0:T(8,128)S(1)} %get-tuple-element.27), channel_id=1, source_target_pairs={{0,2},{2,4},{4,6},{1,3},{3,5},{5,7},{8,10},{10,12},{12,14},{9,11},... | collective-permute-start | bytes 983048 | tf_op jit(solution)/shard_map/ppermute | solution.py:15
  64.5 17.1 %collective-permute-start.5 = (f32[5,2,64,128]{3,2,1,0:T(8,128)S(1)}, f32[5,2,64,128]{3,2,1,0:T(8,128)S(1)}, u32[]{:S(2)}, u32[]{:S(2)}) collective-permute-start(f32[5,2,64,128]{3,2,1,0:T(8,128)S(1)} %get-tuple-element.28), channel_id=1, source_target_pairs={{2,0},{4,2},{6,4},{3,1},{5,3},{7,5},{10,8},{12,10},{14,12},{11,9},... | collective-permute-start | bytes 983048 | tf_op jit(solution)/shard_map/ppermute | solution.py:18
  81.6 2.7 %collective-permute-start.6 = (f32[5,8,2,128]{3,2,1,0:T(2,128)S(1)}, f32[5,8,2,128]{3,2,1,0:T(2,128)S(1)}, u32[]{:S(2)}, u32[]{:S(2)}) collective-permute-start(f32[5,8,2,128]{3,2,1,0:T(2,128)S(1)} %get-tuple-element.23), channel_id=1, source_target_pairs={{0,1},{2,3},{4,5},{6,7},{8,9},{10,11},{12,13},{14,15},{16,17},{18,... | collective-permute-start | bytes 122888 | tf_op jit(solution)/shard_map/ppermute | solution.py:15
  82.9 3.1 %collective-permute-start.7 = (f32[5,8,2,128]{3,2,1,0:T(2,128)S(1)}, f32[5,8,2,128]{3,2,1,0:T(2,128)S(1)}, u32[]{:S(2)}, u32[]{:S(2)}) collective-permute-start(f32[5,8,2,128]{3,2,1,0:T(2,128)S(1)} %get-tuple-element.24), channel_id=1, source_target_pairs={{1,0},{3,2},{5,4},{7,6},{9,8},{11,10},{13,12},{15,14},{17,16},{19,... | collective-permute-start | bytes 122888 | tf_op jit(solution)/shard_map/ppermute | solution.py:18
where the time goes:
time: 89.3 us; the launch traced here: 89 us
  blocking collectives  46 us (52%)
  waiting for transfers between devices  19.2 us (22%)
  starting transfers between devices  15.7 us (18%)
  other arithmetic  6.98 us (8%)
    all_gather x1, blocking collectives, body(): lax.all_gather(velocity, 'trc', axis=3, tiled=True)  16.4 us
    all_gather x1, blocking collectives, body(): lax.all_gather(diffusivity, 'trc', axis=2, tiled=True)  15.8 us
    all_gather x1, blocking collectives, body(): lax.all_gather(upwelling, 'trc', axis=2, tiled=True)  13.8 us
    ppermute x4, waiting for transfers between devices, with_halo(): lax.ppermute(lax.slice_in_dim(block, 0, width, axis=dim), axis, backward)  13.3 us
    ppermute x4, starting transfers between devices, with_halo(): lax.ppermute(lax.slice_in_dim(block, block.shape[dim] - width, None, axis...  10.6 us
    ppermute x4, waiting for transfers between devices, with_halo(): lax.ppermute(lax.slice_in_dim(block, block.shape[dim] - width, None, axis...  5.93 us
    ppermute x4, starting transfers between devices, with_halo(): lax.ppermute(lax.slice_in_dim(block, 0, width, axis=dim), axis, backward)  5.17 us
    mul x6, other arithmetic, face_divergence(): face_flux = face_area * (face_speed * face_value - face_mixing * jump)  2.82 us
  transfers between devices with their start and end apart: 8, of which 4 were waited for; matrix products, arithmetic and copies ran while one was open for 0% of the time, Pallas kernels for 0%

commit v1 on v0

--- a/solution.py
+++ b/solution.py
@@ -5,6 +5,24 @@
 
 STEPS = 2
 fraction_floor = 0.25
+
+
+def collect(value, axis, dim):
+    ways, here, step = (lax.axis_size(axis), lax.axis_index(axis), value.shape[dim])
+    lengths = [n * ways if d == dim else n for d, n in enumerate(value.shape)]
+    full = lax.dynamic_update_slice_in_dim(
+        jnp.zeros(lengths, value.dtype), value, here * step, axis=dim
+    )
+    going_up = going_down = value
+    for far in range(1, ways // 2 + 1):
+        going_up = lax.ppermute(going_up, axis, [(d, (d + 1) % ways) for d in range(ways)])
+        full = lax.dynamic_update_slice_in_dim(full, going_up, (here - far) % ways * step, axis=dim)
+        if 2 * far < ways:
+            going_down = lax.ppermute(going_down, axis, [(d, (d - 1) % ways) for d in range(ways)])
+            full = lax.dynamic_update_slice_in_dim(
+                full, going_down, (here + far) % ways * step, axis=dim
+            )
+    return full
 
 
 def with_halo(block, sides, width):
@@ -83,7 +101,7 @@
     tracer_count = tracers.shape[0]
     collected = []
     moved = (
-        lax.all_gather(velocity, "trc", axis=3, tiled=True),
+        collect(velocity, "trc", 3),
         lax.all_gather(upwelling, "trc", axis=2, tiled=True),
         lax.all_gather(diffusivity, "trc", axis=2, tiled=True),
     )

time: 89.3 us -> 95.7 us (1.072)
  blocking collectives: 46 us -> 29.3 us
  waiting for transfers between devices: 19.2 us -> 33.6 us
  starting transfers between devices: 15.7 us -> 21.4 us
  local copies, waits for them, and re-layouts: 0.57 us -> 3.43 us
    all_gather x1 -> x0, blocking collectives: 16.4 us -> none  [body(): lax.all_gather(velocity, 'trc', axis=3, tiled=True)]
    ppermute x0 -> x3, starting transfers between devices: none -> 6.6 us  [the longest x1 5.1 us: collect(): lax.ppermute(going_down, axis, [(d, (d - 1) % ways) for d in range(ways)])]
    ppermute x4, waiting for transfers between devices: 13.3 us -> 18.8 us  [with_halo(): lax.ppermute(lax.slice_in_dim(block, 0, width, axis=dim), axis, backward)]
    ppermute x0 -> x3, waiting for transfers between devices: none -> 5.04 us  [the longest x2 5.04 us: collect(): lax.ppermute(going_up, axis, [(d, (d + 1) % ways) for d in range(ways)])]
    ppermute x4, waiting for transfers between devices: 5.93 us -> 9.83 us  [with_halo(): lax.ppermute(lax.slice_in_dim(block, block.shape[dim] - width, None, axis...]
    unnamed x9 -> x11, local copies, waits for them, and re-layouts: 0.05 us -> 1.85 us
    all_gather x1, blocking collectives: 15.8 us -> 14.4 us  [body(): lax.all_gather(diffusivity, 'trc', axis=2, tiled=True)]
    all_gather x1, blocking collectives: 13.8 us -> 14.9 us  [body(): lax.all_gather(upwelling, 'trc', axis=2, tiled=True)]
  transfers between devices with their start and end apart: 8 -> 11, of which waited for: 4 -> 7; matrix products, arithmetic and copies ran while one was open for 0% -> 3% of each run, Pallas kernels for 0% -> 0%
where the time goes in v1:
time: 95.7 us; the launch traced here: 95.3 us
  waiting for transfers between devices  33.6 us (35%)
  blocking collectives  29.3 us (31%)
  starting transfers between devices  21.4 us (22%)
  other arithmetic  6.95 us (7%)
  local copies, waits for them, and re-layouts  3.43 us (4%)
    ppermute x4, waiting for transfers between devices, with_halo(): lax.ppermute(lax.slice_in_dim(block, 0, width, axis=dim), axis, backward)  18.8 us
    all_gather x1, blocking collectives, body(): lax.all_gather(upwelling, 'trc', axis=2, tiled=True)  14.9 us
    all_gather x1, blocking collectives, body(): lax.all_gather(diffusivity, 'trc', axis=2, tiled=True)  14.4 us
    ppermute x4, waiting for transfers between devices, with_halo(): lax.ppermute(lax.slice_in_dim(block, block.shape[dim] - width, None, axis...  9.83 us
    ppermute x4, starting transfers between devices, with_halo(): lax.ppermute(lax.slice_in_dim(block, block.shape[dim] - width, None, axis...  9.68 us
    ppermute x4, starting transfers between devices, with_halo(): lax.ppermute(lax.slice_in_dim(block, 0, width, axis=dim), axis, backward)  5.17 us
    ppermute x1, starting transfers between devices, collect(): lax.ppermute(going_down, axis, [(d, (d - 1) % ways) for d in range(ways)])  5.1 us
    ppermute x2, waiting for transfers between devices, collect(): lax.ppermute(going_up, axis, [(d, (d + 1) % ways) for d in range(ways)])  5.04 us
  transfers between devices with their start and end apart: 11, of which 7 were waited for; matrix products, arithmetic and copies ran while one was open for 3% of the time, Pallas kernels for 0%

profile of v1, /device:TPU:0, one launch (start us, length us, event | category | flops | bytes accessed | tf_op | source)
XLA Modules:
  0.0 95.3 jit_solution(10690436065592188077)
XLA Ops:
  0.0 5.1 %collective-permute-start.1 = (f32[2,2,1,8192]{3,2,1,0:T(1,128)}, f32[2,2,1,8192]{3,2,1,0:T(1,128)S(1)}, u32[]{:S(2)}, u32[]{:S(2)}) collective-permute-start(f32[2,2,1,8192]{3,2,1,0:T(1,128)} %param.11), channel_id=1, source_target_pairs={{0,24},{8,0},{16,8},{24,16},{1,25},{9,1},{17,9},{25,17},{2,26},{10... | collective-permute-start | bytes 393224 | tf_op jit(solution)/shard_map/ppermute | solution.py:21
  6.5 14.4 %all_gather.6 = f32[2,1,32768]{2,1,0:T(1,128)S(1)} all-gather(f32[2,1,8192]{2,1,0:T(1,128)} %param.13), channel_id=1, replica_groups=mesh['trc'=4,'lat'=4,'lon'=2] {'trc'}, dimensions={2}, use_global_device_ids=true | all-gather | bytes 327680 | tf_op jit(solution)/shard_map/all_gather | solution.py:106
  20.9 1.0 %constant_dynamic-update-slice_fusion.1 = f32[6,4,64,128]{3,2,1,0:T(8,128)S(1)} fusion(f32[2,4,64,128]{3,2,1,0:T(8,128)} %param.7), kind=kLoop, calls=%fused_computation.126 | loop fusion | bytes 524288
  22.4 14.9 %all_gather.7 = f32[2,1,32768]{2,1,0:T(1,128)S(1)} all-gather(f32[2,1,8192]{2,1,0:T(1,128)S(1)} %copy-done.2), channel_id=1, replica_groups=mesh['trc'=4,'lat'=4,'lon'=2] {'trc'}, dimensions={2}, use_global_device_ids=true | all-gather | bytes 327680 | tf_op jit(solution)/shard_map/all_gather | solution.py:105
  37.3 1.5 %collective-permute-start.2 = (f32[2,2,1,8192]{3,2,1,0:T(1,128)S(1)}, f32[2,2,1,8192]{3,2,1,0:T(1,128)S(1)}, u32[]{:S(2)}, u32[]{:S(2)}) collective-permute-start(f32[2,2,1,8192]{3,2,1,0:T(1,128)S(1)} %collective-permute-done), channel_id=1, source_target_pairs={{0,8},{8,16},{16,24},{24,0},{1,9},{9,17},{17,25},{25,1},{2,10},{10... | collective-permute-start | bytes 393224 | tf_op jit(solution)/shard_map/ppermute | solution.py:18
  39.0 5.0 %collective-permute-done.2 = f32[2,2,1,8192]{3,2,1,0:T(1,128)S(1)} collective-permute-done((f32[2,2,1,8192]{3,2,1,0:T(1,128)S(1)}, f32[2,2,1,8192]{3,2,1,0:T(1,128)S(1)}, u32[]{:S(2)}, u32[]{:S(2)}) %collective-permute-start.2) | collective-permute-done | bytes 131104 | tf_op jit(solution)/shard_map/ppermute | solution.py:18
  44.8 3.4 %collective-permute-start.3 = (f32[6,2,64,128]{3,2,1,0:T(8,128)S(1)}, f32[6,2,64,128]{3,2,1,0:T(8,128)S(1)}, u32[]{:S(2)}, u32[]{:S(2)}) collective-permute-start(f32[6,2,64,128]{3,2,1,0:T(8,128)S(1)} %get-tuple-element.25), channel_id=1, source_target_pairs={{0,2},{2,4},{4,6},{1,3},{3,5},{5,7},{8,10},{10,12},{12,14},{9,11},... | collective-permute-start | bytes 1179656 | tf_op jit(solution)/shard_map/ppermute | solution.py:33
  48.2 1.3 %collective-permute-start.4 = (f32[6,2,64,128]{3,2,1,0:T(8,128)S(1)}, f32[6,2,64,128]{3,2,1,0:T(8,128)S(1)}, u32[]{:S(2)}, u32[]{:S(2)}) collective-permute-start(f32[6,2,64,128]{3,2,1,0:T(8,128)S(1)} %get-tuple-element.26), channel_id=1, source_target_pairs={{2,0},{4,2},{6,4},{3,1},{5,3},{7,5},{10,8},{12,10},{14,12},{11,9},... | collective-permute-start | bytes 1179656 | tf_op jit(solution)/shard_map/ppermute | solution.py:36
  49.6 3.9 %collective-permute-done.3 = f32[6,2,64,128]{3,2,1,0:T(8,128)S(1)} collective-permute-done((f32[6,2,64,128]{3,2,1,0:T(8,128)S(1)}, f32[6,2,64,128]{3,2,1,0:T(8,128)S(1)}, u32[]{:S(2)}, u32[]{:S(2)}) %collective-permute-start.3) | collective-permute-done | bytes 393248 | tf_op jit(solution)/shard_map/ppermute | solution.py:33
  53.5 7.6 %collective-permute-done.4 = f32[6,2,64,128]{3,2,1,0:T(8,128)S(1)} collective-permute-done((f32[6,2,64,128]{3,2,1,0:T(8,128)S(1)}, f32[6,2,64,128]{3,2,1,0:T(8,128)S(1)}, u32[]{:S(2)}, u32[]{:S(2)}) %collective-permute-start.4) | collective-permute-done | bytes 393248 | tf_op jit(solution)/shard_map/ppermute | solution.py:36
  61.1 1.3 %collective-permute-start.5 = (f32[6,8,2,128]{3,2,1,0:T(2,128)S(1)}, f32[6,8,2,128]{3,2,1,0:T(2,128)S(1)}, u32[]{:S(2)}, u32[]{:S(2)}) collective-permute-start(f32[6,8,2,128]{3,2,1,0:T(2,128)S(1)} %get-tuple-element.16), channel_id=1, source_target_pairs={{0,1},{2,3},{4,5},{6,7},{8,9},{10,11},{12,13},{14,15},{16,17},{18,... | collective-permute-start | bytes 147464 | tf_op jit(solution)/shard_map/ppermute | solution.py:33
  62.4 1.3 %collective-permute-start.6 = (f32[6,8,2,128]{3,2,1,0:T(2,128)S(1)}, f32[6,8,2,128]{3,2,1,0:T(2,128)S(1)}, u32[]{:S(2)}, u32[]{:S(2)}) collective-permute-start(f32[6,8,2,128]{3,2,1,0:T(2,128)S(1)} %get-tuple-element.17), channel_id=1, source_target_pairs={{1,0},{3,2},{5,4},{7,6},{9,8},{11,10},{13,12},{15,14},{17,16},{19,... | collective-permute-start | bytes 147464 | tf_op jit(solution)/shard_map/ppermute | solution.py:36
  63.7 1.8 %collective-permute-done.6 = f32[6,8,2,128]{3,2,1,0:T(2,128)S(1)} collective-permute-done((f32[6,8,2,128]{3,2,1,0:T(2,128)S(1)}, f32[6,8,2,128]{3,2,1,0:T(2,128)S(1)}, u32[]{:S(2)}, u32[]{:S(2)}) %collective-permute-start.6) | collective-permute-done | bytes 49184 | tf_op jit(solution)/shard_map/ppermute | solution.py:36
  66.7 1.0 %subtract_multiply_fusion.1 = f32[2,8,65,128]{3,2,1,0:T(8,128)S(1)} fusion(f32[6,8,2,128]{3,2,1,0:T(2,128)S(1)} %collective-permute-done.6, f32[6,2,64,128]{3,2,1,0:T(8,128)S(1)} %collective-permute-done.4, f32[6,4,64,128]{3,2,1,0:T(8,128)S(1)} %constant_dynamic-update-slice_fusion, f32[6,2,64,128]{3,2,1,0:T(8,128)S(1)} %collective-permute-done.3, ...), kind=kLoop, calls=%fused_computation.33 | loop fusion | flops 5058560 | bytes 3335168 | tf_op jit(solution)/shard_map/mul | solution.py:67
  67.9 0.8 copy-done
  69.2 3.4 %collective-permute-start.7 = (f32[5,2,64,128]{3,2,1,0:T(8,128)S(1)}, f32[5,2,64,128]{3,2,1,0:T(8,128)S(1)}, u32[]{:S(2)}, u32[]{:S(2)}) collective-permute-start(f32[5,2,64,128]{3,2,1,0:T(8,128)S(1)} %get-tuple-element.27), channel_id=1, source_target_pairs={{0,2},{2,4},{4,6},{1,3},{3,5},{5,7},{8,10},{10,12},{12,14},{9,11},... | collective-permute-start | bytes 983048 | tf_op jit(solution)/shard_map/ppermute | solution.py:33
  72.6 1.3 %collective-permute-start.8 = (f32[5,2,64,128]{3,2,1,0:T(8,128)S(1)}, f32[5,2,64,128]{3,2,1,0:T(8,128)S(1)}, u32[]{:S(2)}, u32[]{:S(2)}) collective-permute-start(f32[5,2,64,128]{3,2,1,0:T(8,128)S(1)} %get-tuple-element.28), channel_id=1, source_target_pairs={{2,0},{4,2},{6,4},{3,1},{5,3},{7,5},{10,8},{12,10},{14,12},{11,9},... | collective-permute-start | bytes 983048 | tf_op jit(solution)/shard_map/ppermute | solution.py:36
  73.9 5.9 %collective-permute-done.7 = f32[5,2,64,128]{3,2,1,0:T(8,128)S(1)} collective-permute-done((f32[5,2,64,128]{3,2,1,0:T(8,128)S(1)}, f32[5,2,64,128]{3,2,1,0:T(8,128)S(1)}, u32[]{:S(2)}, u32[]{:S(2)}) %collective-permute-start.7) | collective-permute-done | bytes 327712 | tf_op jit(solution)/shard_map/ppermute | solution.py:33
  79.8 7.8 %collective-permute-done.8 = f32[5,2,64,128]{3,2,1,0:T(8,128)S(1)} collective-permute-done((f32[5,2,64,128]{3,2,1,0:T(8,128)S(1)}, f32[5,2,64,128]{3,2,1,0:T(8,128)S(1)}, u32[]{:S(2)}, u32[]{:S(2)}) %collective-permute-start.8) | collective-permute-done | bytes 327712 | tf_op jit(solution)/shard_map/ppermute | solution.py:36
  87.7 1.6 %collective-permute-start.9 = (f32[5,8,2,128]{3,2,1,0:T(2,128)S(1)}, f32[5,8,2,128]{3,2,1,0:T(2,128)S(1)}, u32[]{:S(2)}, u32[]{:S(2)}) collective-permute-start(f32[5,8,2,128]{3,2,1,0:T(2,128)S(1)} %get-tuple-element.23), channel_id=1, source_target_pairs={{0,1},{2,3},{4,5},{6,7},{8,9},{10,11},{12,13},{14,15},{16,17},{18,... | collective-permute-start | bytes 122888 | tf_op jit(solution)/shard_map/ppermute | solution.py:33
  89.2 1.3 %collective-permute-start.10 = (f32[5,8,2,128]{3,2,1,0:T(2,128)S(1)}, f32[5,8,2,128]{3,2,1,0:T(2,128)S(1)}, u32[]{:S(2)}, u32[]{:S(2)}) collective-permute-start(f32[5,8,2,128]{3,2,1,0:T(2,128)S(1)} %get-tuple-element.24), channel_id=1, source_target_pairs={{1,0},{3,2},{5,4},{7,6},{9,8},{11,10},{13,12},{15,14},{17,16},{19,... | collective-permute-start | bytes 122888 | tf_op jit(solution)/shard_map/ppermute | solution.py:36
  90.7 1.7 %collective-permute-done.10 = f32[5,8,2,128]{3,2,1,0:T(2,128)S(1)} collective-permute-done((f32[5,8,2,128]{3,2,1,0:T(2,128)S(1)}, f32[5,8,2,128]{3,2,1,0:T(2,128)S(1)}, u32[]{:S(2)}, u32[]{:S(2)}) %collective-permute-start.10) | collective-permute-done | bytes 40992 | tf_op jit(solution)/shard_map/ppermute | solution.py:36
  93.3 1.0 %subtract_multiply_fusion = f32[2,8,65,128]{3,2,1,0:T(8,128)S(1)} fusion(f32[5,8,2,128]{3,2,1,0:T(2,128)S(1)} %collective-permute-done.10, f32[5,2,64,128]{3,2,1,0:T(8,128)S(1)} %collective-permute-done.8, f32[1,4,64,128]{3,2,1,0:T(8,128)S(1)} %bitcast.49, f32[1,4,64,128]{3,2,1,0:T(8,128)S(1)} %get-tuple-element.34, ...), kind=kLoop, calls=%fused_computation.29 | loop fusion | flops 6656000 | bytes 3056640 | tf_op jit(solution)/shard_map/mul | solution.py:67
  94.4 0.9 fusion.20
  (59 shorter events, 5.7 us)
Async XLA Ops:
  0.0 22.0 %copy-start.1 = (f32[2,2,1,8192]{3,2,1,0:T(1,128)S(1)}, f32[2,2,1,8192]{3,2,1,0:T(1,128)}, u32[]{:S(2)}) copy-start(f32[2,2,1,8192]{3,2,1,0:T(1,128)} %param.11) | copy-start | bytes 393220
  0.0 22.1 %copy-start.3 = (f32[4,64]{1,0:T(4,128)S(1)}, f32[4,64]{1,0:T(4,128)}, u32[]{:S(2)}) copy-start(f32[4,64]{1,0:T(4,128)} %param.10) | copy-start | bytes 3076
  0.0 22.4 %copy-start.2 = (f32[2,1,8192]{2,1,0:T(1,128)S(1)}, f32[2,1,8192]{2,1,0:T(1,128)}, u32[]{:S(2)}) copy-start(f32[2,1,8192]{2,1,0:T(1,128)} %param.12) | copy-start | bytes 196612
  0.0 38.9 %collective-permute-start.1 = (f32[2,2,1,8192]{3,2,1,0:T(1,128)}, f32[2,2,1,8192]{3,2,1,0:T(1,128)S(1)}, u32[]{:S(2)}, u32[]{:S(2)}) collective-permute-start(f32[2,2,1,8192]{3,2,1,0:T(1,128)} %param.11), channel_id=1, source_target_pairs={{0,24},{8,0},{16,8},{24,16},{1,25},{9,1},{17,9},{25,17},{2,26},{10... | collective-permute-start | bytes 393224 | tf_op jit(solution)/shard_map/ppermute | solution.py:21
  5.1 32.2 %collective-permute-start = (f32[2,2,1,8192]{3,2,1,0:T(1,128)}, f32[2,2,1,8192]{3,2,1,0:T(1,128)S(1)}, u32[]{:S(2)}, u32[]{:S(2)}) collective-permute-start(f32[2,2,1,8192]{3,2,1,0:T(1,128)} %param.11), channel_id=1, source_target_pairs={{0,8},{8,16},{16,24},{24,0},{1,9},{9,17},{17,25},{25,1},{2,10},{10... | collective-permute-start | bytes 393224 | tf_op jit(solution)/shard_map/ppermute | solution.py:18
  37.3 6.8 %collective-permute-start.2 = (f32[2,2,1,8192]{3,2,1,0:T(1,128)S(1)}, f32[2,2,1,8192]{3,2,1,0:T(1,128)S(1)}, u32[]{:S(2)}, u32[]{:S(2)}) collective-permute-start(f32[2,2,1,8192]{3,2,1,0:T(1,128)S(1)} %collective-permute-done), channel_id=1, source_target_pairs={{0,8},{8,16},{16,24},{24,0},{1,9},{9,17},{17,25},{25,1},{2,10},{10... | collective-permute-start | bytes 393224 | tf_op jit(solution)/shard_map/ppermute | solution.py:18
  44.8 8.7 %collective-permute-start.3 = (f32[6,2,64,128]{3,2,1,0:T(8,128)S(1)}, f32[6,2,64,128]{3,2,1,0:T(8,128)S(1)}, u32[]{:S(2)}, u32[]{:S(2)}) collective-permute-start(f32[6,2,64,128]{3,2,1,0:T(8,128)S(1)} %get-tuple-element.25), channel_id=1, source_target_pairs={{0,2},{2,4},{4,6},{1,3},{3,5},{5,7},{8,10},{10,12},{12,14},{9,11},... | collective-permute-start | bytes 1179656 | tf_op jit(solution)/shard_map/ppermute | solution.py:33
  48.2 12.8 %collective-permute-start.4 = (f32[6,2,64,128]{3,2,1,0:T(8,128)S(1)}, f32[6,2,64,128]{3,2,1,0:T(8,128)S(1)}, u32[]{:S(2)}, u32[]{:S(2)}) collective-permute-start(f32[6,2,64,128]{3,2,1,0:T(8,128)S(1)} %get-tuple-element.26), channel_id=1, source_target_pairs={{2,0},{4,2},{6,4},{3,1},{5,3},{7,5},{10,8},{12,10},{14,12},{11,9},... | collective-permute-start | bytes 1179656 | tf_op jit(solution)/shard_map/ppermute | solution.py:36
  61.1 2.6 %collective-permute-start.5 = (f32[6,8,2,128]{3,2,1,0:T(2,128)S(1)}, f32[6,8,2,128]{3,2,1,0:T(2,128)S(1)}, u32[]{:S(2)}, u32[]{:S(2)}) collective-permute-start(f32[6,8,2,128]{3,2,1,0:T(2,128)S(1)} %get-tuple-element.16), channel_id=1, source_target_pairs={{0,1},{2,3},{4,5},{6,7},{8,9},{10,11},{12,13},{14,15},{16,17},{18,... | collective-permute-start | bytes 147464 | tf_op jit(solution)/shard_map/ppermute | solution.py:33
  62.4 3.1 %collective-permute-start.6 = (f32[6,8,2,128]{3,2,1,0:T(2,128)S(1)}, f32[6,8,2,128]{3,2,1,0:T(2,128)S(1)}, u32[]{:S(2)}, u32[]{:S(2)}) collective-permute-start(f32[6,8,2,128]{3,2,1,0:T(2,128)S(1)} %get-tuple-element.17), channel_id=1, source_target_pairs={{1,0},{3,2},{5,4},{7,6},{9,8},{11,10},{13,12},{15,14},{17,16},{19,... | collective-permute-start | bytes 147464 | tf_op jit(solution)/shard_map/ppermute | solution.py:36
  67.8 1.0 %copy-start = (f32[2,4,64,128]{3,2,1,0:T(8,128)S(1)}, f32[2,4,64,128]{3,2,1,0:T(8,128)}, u32[]{:S(2)}) copy-start(f32[2,4,64,128]{3,2,1,0:T(8,128)} %param.7) | copy-start | bytes 786436
  69.2 10.7 %collective-permute-start.7 = (f32[5,2,64,128]{3,2,1,0:T(8,128)S(1)}, f32[5,2,64,128]{3,2,1,0:T(8,128)S(1)}, u32[]{:S(2)}, u32[]{:S(2)}) collective-permute-start(f32[5,2,64,128]{3,2,1,0:T(8,128)S(1)} %get-tuple-element.27), channel_id=1, source_target_pairs={{0,2},{2,4},{4,6},{1,3},{3,5},{5,7},{8,10},{10,12},{12,14},{9,11},... | collective-permute-start | bytes 983048 | tf_op jit(solution)/shard_map/ppermute | solution.py:33
  72.6 15.0 %collective-permute-start.8 = (f32[5,2,64,128]{3,2,1,0:T(8,128)S(1)}, f32[5,2,64,128]{3,2,1,0:T(8,128)S(1)}, u32[]{:S(2)}, u32[]{:S(2)}) collective-permute-start(f32[5,2,64,128]{3,2,1,0:T(8,128)S(1)} %get-tuple-element.28), channel_id=1, source_target_pairs={{2,0},{4,2},{6,4},{3,1},{5,3},{7,5},{10,8},{12,10},{14,12},{11,9},... | collective-permute-start | bytes 983048 | tf_op jit(solution)/shard_map/ppermute | solution.py:36
  87.7 3.0 %collective-permute-start.9 = (f32[5,8,2,128]{3,2,1,0:T(2,128)S(1)}, f32[5,8,2,128]{3,2,1,0:T(2,128)S(1)}, u32[]{:S(2)}, u32[]{:S(2)}) collective-permute-start(f32[5,8,2,128]{3,2,1,0:T(2,128)S(1)} %get-tuple-element.23), channel_id=1, source_target_pairs={{0,1},{2,3},{4,5},{6,7},{8,9},{10,11},{12,13},{14,15},{16,17},{18,... | collective-permute-start | bytes 122888 | tf_op jit(solution)/shard_map/ppermute | solution.py:33
  89.2 3.1 %collective-permute-start.10 = (f32[5,8,2,128]{3,2,1,0:T(2,128)S(1)}, f32[5,8,2,128]{3,2,1,0:T(2,128)S(1)}, u32[]{:S(2)}, u32[]{:S(2)}) collective-permute-start(f32[5,8,2,128]{3,2,1,0:T(2,128)S(1)} %get-tuple-element.24), channel_id=1, source_target_pairs={{1,0},{3,2},{5,4},{7,6},{9,8},{11,10},{13,12},{15,14},{17,16},{19,... | collective-permute-start | bytes 122888 | tf_op jit(solution)/shard_map/ppermute | solution.py:36
